TPU v7x, 32 devices: a whole 2x2x4 slice. The times are simulated.
32 devices in a mesh: pair: 2 (over core), vcol: 16 (over z, y, x).
Axes of the slice: x: 2, y: 2, z: 4, core: 2. Of those that a mesh axis runs over, the one named last changes fastest.
Arguments:
- amplitudes: bfloat16 [1280, 4096], P('pair', 'vcol'), may hold values from -6 to 6
- tile_owner: int32 [32], replicated, may hold values from 0 to 31, each once
- integrals: bfloat16 [4096, 4096], P('pair', 'vcol'), may hold values from -0.125 to 0.125
- screening: int32 [20, 32, 32], P('pair'), may hold values 0 or 1
- occ_energy: float32 [1280], P('pair'), may hold values from -1 to -0.2
- virt_energy: float32 [4096], replicated, may hold values from 0.2 to 1
Outputs:
- residual: bfloat16 [1280, 4096], P('pair', 'vcol')
Inputs may be any that keep to these rules, and one draw needn't show every extreme that they name: `tile_owner`: each of the 32 tiles appears exactly once.
All inputs are finite; a program needn't handle non-finite values. No bound on the sum of `screening` on one device may be relied on, other than what follows from the above.
Results may differ from a plain program's by a relative error of at most 0.0036.
Values may be sent and summed in bfloat16 or wider, within the bound.
A program may use at most 64 MiB of HBM per device.

v0:
```python
import jax
import jax.numpy as jnp
from jax import lax
from jax.sharding import PartitionSpec as P

TILE = 128
PBLK = 64
KT_DEV = 2


def one_hot(indices, length):
    return (indices[:, None] == jnp.arange(length, dtype=jnp.int32)[None, :]).astype(jnp.float32)


def gather_rows(panel):
    return lax.all_gather(panel, "pair", axis=0, tiled=True)


def local(amplitudes, tile_owner, integrals, screening, occ_energy, virt_energy):
    pair_local = amplitudes.shape[0]
    tile_count = tile_owner.shape[0]
    width = KT_DEV * TILE
    block_count = pair_local // PBLK
    column = lax.axis_index("vcol")
    first_slot = column * KT_DEV
    owned_tiles = lax.dynamic_slice_in_dim(tile_owner, first_slot, KT_DEV, 0)
    screen_float = screening.astype(jnp.float32)
    natural_tiles = first_slot + jnp.arange(KT_DEV, dtype=jnp.int32)
    panel = gather_rows(integrals)
    picked = jnp.einsum("bct,jt->bcj", screen_float, one_hot(natural_tiles, tile_count))
    marks_slot = jnp.take(picked, tile_owner, axis=1).astype(jnp.bfloat16)
    panel_slot = jnp.take(panel.reshape(tile_count, TILE, width), tile_owner, axis=0)
    piece_in = lax.all_gather(amplitudes, "vcol", axis=1, tiled=True)
    tiles_in = piece_in.shape[1] // TILE
    left_all = piece_in.reshape(block_count, PBLK, tiles_in * TILE)

    def one_block(operands):
        left_rows, marks = operands
        masked = (
            panel_slot.reshape(tiles_in, TILE, KT_DEV, TILE) * marks[:, None, :, None]
        ).reshape(tiles_in * TILE, width)
        return jnp.dot(left_rows, masked, preferred_element_type=jnp.float32)

    summed = lax.map(one_block, (left_all, marks_slot))
    ladder_local = summed.reshape(pair_local, width).astype(jnp.bfloat16)
    piece_in = lax.all_gather(ladder_local, "vcol", axis=1, tiled=True)
    tiles_in = piece_in.shape[1] // TILE
    chooser = one_hot(owned_tiles, tiles_in).astype(jnp.bfloat16)
    shaped = piece_in.reshape(piece_in.shape[0], tiles_in, TILE)
    ladder_owned = jnp.einsum(
        "pmk,jm->pjk", shaped, chooser, preferred_element_type=jnp.float32
    ).reshape(pair_local, width)
    virt_owned = jnp.dot(
        one_hot(owned_tiles, tile_count),
        virt_energy.reshape(tile_count, TILE),
        precision=lax.Precision.HIGHEST,
    ).reshape(width)
    residual = ladder_owned + (virt_owned[None, :] - occ_energy[:, None]) * amplitudes.astype(
        jnp.float32
    )
    return residual.astype(jnp.bfloat16)


def solution(mesh):
    return jax.shard_map(
        local,
        mesh=mesh,
        in_specs=(P("pair", "vcol"), P(), P("pair", "vcol"), P("pair", None, None), P("pair"), P()),
        out_specs=P("pair", "vcol"),
        check_vma=False,
    )
```

profile of v0, /device:TPU:0, one launch (start us, length us, event | category | flops | bytes accessed | tf_op | source)
XLA Modules:
  0.0 258.9 jit_solution(7271926033626075725)
XLA Ops:
  6.5 0.7 all-gather.6.cloned.1.call-update
  7.3 0.7 all-gather.4.cloned.1.call-update
  8.1 1.2 convolution_bitcast_fusion.1
  9.4 0.7 compare_select_fusion
  10.7 0.7 compare_and_fusion
  11.5 10.7 %all-gather.6.cloned.1.call-done = bf16[4096,256]{1,0:T(8,128)(2,1)} async-done(((bf16[2048,256]{1,0:T(8,128)(2,1)}), bf16[4096,256]{1,0:T(8,128)(2,1)}) %all-gather.6.cloned.1.call-update) | async-done | bytes 2097168 | tf_op jit(solution)/shard_map/all_gather | solution.py:16
  22.2 3.7 %gather_fusion.1 = bf16[32,128,256]{2,1,0:T(8,128)(2,1)} fusion(bf16[32,128,256]{2,1,0:T(8,128)(2,1)} %bitcast.60, s32[1024]{0:T(1024)S(1)} %pad_clamp_fusion), kind=kCustom, calls=%fused_computation.1 | custom fusion | bytes 4194432 | tf_op jit(solution)/shard_map/jit(_take)/gather | solution.py:32
  25.9 1.8 broadcast_select_fusion
  27.7 96.8 %all-gather.4.cloned.1.call-done = bf16[640,4096]{1,0:T(8,128)(2,1)} async-done(((bf16[640,256]{1,0:T(8,128)(2,1)}), bf16[640,4096]{1,0:T(8,128)(2,1)}) %all-gather.4.cloned.1.call-update) | async-done | bytes 5242896 | tf_op jit(solution)/shard_map/all_gather | solution.py:33
  124.5 25.2 %while.10 = (s32[]{:T(128)}, bf16[10,64,256]{2,1,0:T(8,128)(2,1)}, bf16[10,64,4096]{2,1,0:T(8,128)(2,1)}, bf16[10,32,2]{1,2,0:T(2,128)(2,1)S(1)}, bf16[32,128,256]{2,1,0:T(8,128)(2,1)S(1)}, /*index=5*/s32[]{:T(128)}) while((s32[]{:T(128)}, bf16[10,64,256]{2,1,0:T(8,128)(2,1)}, bf16[10,64,4096]{2,1,0:T(8,128)(2,1)}, ...), condition=%wide.region_1.2_spmd, body=%wide.region_0.1_spmd.sunk | while | flops 135266304 | bytes 6948553 | solution.py:44
  124.9 2.1 fusion.27
  127.4 2.1 fusion.27
  129.9 2.1 fusion.27
  132.4 2.1 fusion.27
  135.0 2.1 fusion.27
  137.5 2.1 fusion.27
  140.0 2.1 fusion.27
  142.5 2.1 fusion.27
  145.0 2.1 fusion.27
  147.5 2.1 fusion.27
  150.0 96.4 %all-gather.8.cloned.1.call-done = bf16[640,4096]{1,0:T(8,128)(2,1)} async-done(((bf16[640,256]{1,0:T(8,128)(2,1)}), bf16[640,4096]{1,0:T(8,128)(2,1)}) %all-gather.8.cloned.1.call-update) | async-done | bytes 5242896 | tf_op jit(solution)/shard_map/all_gather | solution.py:46
  246.4 4.1 %copy.12 = bf16[80,8,32,128]{3,2,1,0:T(8,128)(2,1)S(1)} copy(bf16[80,8,32,128]{3,1,2,0:T(8,128)(2,1)} %bitcast.58) | data formatting | bytes 10485760
  250.6 0.9 fusion.13
  251.5 0.9 fusion.5
  (71 shorter events, 5.0 us)
Async XLA Ops:
  6.5 143.3 %copy-start = (f32[4096]{0:T(1024)S(1)}, f32[4096]{0:T(1024)}, u32[]{:S(2)}) copy-start(f32[4096]{0:T(1024)} %param.13) | copy-start | bytes 49156
  6.5 15.7 %all-gather.6.cloned.1.call-start = ((), (), s32[]{:S(2)}) async-start(), calls=%async_computation.1 | async-start | bytes 3145728 | tf_op jit(solution)/shard_map/all_gather | solution.py:16
  7.3 117.2 %all-gather.4.cloned.1.call-start = ((), (), s32[]{:S(2)}) async-start(), calls=%async_computation | async-start | bytes 5570560 | tf_op jit(solution)/shard_map/all_gather | solution.py:33
  8.0 238.4 %all-gather.8.cloned.1.call-start = ((), (), s32[]{:S(2)}) async-start(), calls=%async_computation.2 | async-start | bytes 5570560 | tf_op jit(solution)/shard_map/all_gather | solution.py:46
  124.5 25.2 %copy-start.3 = (s32[32]{0:T(128)S(1)}, s32[32]{0:T(128)}, u32[]{:S(2)}) copy-start(s32[32]{0:T(128)} %param.9) | copy-start | bytes 388
  250.5 1.0 copy-start.1
  250.5 1.0 copy-start.2
Sparse Core Ops, SparseCore 0:
  8.9 13.2 all-gather.5
  24.9 99.5 all-gather.3
  149.8 96.5 all-gather.7
where the time goes:
time: 260 us; the launch traced here: 259 us
  waiting for transfers between devices  205 us (79%)
  matrix products  23.6 us (9%)
  between operations  13.2 us (5%)
  local copies, waits for them, and re-layouts  10.9 us (4%)
  other arithmetic  5.66 us (2%)
    all_gather x1, waiting for transfers between devices, local(): piece_in = lax.all_gather(amplitudes, 'vcol', axis=1, tiled=True)  96.8 us
    all_gather x1, waiting for transfers between devices, local(): piece_in = lax.all_gather(ladder_local, 'vcol', axis=1, tiled=True)  96.4 us
    dot_general x10, matrix products, one_block(): return jnp.dot(left_rows, masked, preferred_element_type=jnp.float32)  21.4 us
    all_gather x1, waiting for transfers between devices, gather_rows(): return lax.all_gather(panel, 'pair', axis=0, tiled=True)  10.7 us
  transfers between devices with their start and end apart: 3, of which 3 were waited for; matrix products, arithmetic and copies ran while one was open for 4% of the time, Pallas kernels for 0%

commit v1 on v0

--- a/solution.py
+++ b/solution.py
@@ -30,7 +30,7 @@
     picked = jnp.einsum("bct,jt->bcj", screen_float, one_hot(natural_tiles, tile_count))
     marks_slot = jnp.take(picked, tile_owner, axis=1).astype(jnp.bfloat16)
     panel_slot = jnp.take(panel.reshape(tile_count, TILE, width), tile_owner, axis=0)
-    piece_in = lax.all_gather(amplitudes, "vcol", axis=1, tiled=True)
+    piece_in = jnp.concatenate(lax.all_gather(amplitudes, "vcol"), axis=1)
     tiles_in = piece_in.shape[1] // TILE
     left_all = piece_in.reshape(block_count, PBLK, tiles_in * TILE)
 

time: 260 us -> 263 us (1.012)
  local copies, waits for them, and re-layouts: 10.9 us -> 27.6 us
  waiting for transfers between devices: 205 us -> 192 us
    all_gather x1, waiting for transfers between devices: 96.8 us -> 82.8 us  [local(): piece_in = jnp.concatenate(lax.all_gather(amplitudes, 'vcol'), axis=1)]
    another operation x0 -> x1, local copies, waits for them, and re-layouts: none -> 8.92 us  [local(): left_all = piece_in.reshape(block_count, PBLK, tiles_in * TILE)]
    all_gather x0 -> x1, local copies, waits for them, and re-layouts: none -> 7.79 us  [local(): piece_in = jnp.concatenate(lax.all_gather(amplitudes, 'vcol'), axis=1)]
where the time goes in v1:
time: 263 us; the launch traced here: 262 us
  waiting for transfers between devices  192 us (73%)
  local copies, waits for them, and re-layouts  27.6 us (10%)
  matrix products  23.5 us (9%)
  between operations  13.2 us (5%)
  other arithmetic  5.66 us (2%)
    all_gather x1, waiting for transfers between devices, local(): piece_in = lax.all_gather(ladder_local, 'vcol', axis=1, tiled=True)  97 us
    all_gather x1, waiting for transfers between devices, local(): piece_in = jnp.concatenate(lax.all_gather(amplitudes, 'vcol'), axis=1)  82.8 us
    dot_general x10, matrix products, one_block(): return jnp.dot(left_rows, masked, preferred_element_type=jnp.float32)  21.4 us
    all_gather x1, waiting for transfers between devices, gather_rows(): return lax.all_gather(panel, 'pair', axis=0, tiled=True)  10.7 us
    another operation x1, local copies, waits for them, and re-layouts, local(): left_all = piece_in.reshape(block_count, PBLK, tiles_in * TILE)  8.92 us
    all_gather x1, local copies, waits for them, and re-layouts, local(): piece_in = jnp.concatenate(lax.all_gather(amplitudes, 'vcol'), axis=1)  7.79 us
  transfers between devices with their start and end apart: 3, of which 3 were waited for; matrix products, arithmetic and copies ran while one was open for 4% of the time, Pallas kernels for 0%

profile of v1, /device:TPU:0, one launch (start us, length us, event | category | flops | bytes accessed | tf_op | source)
XLA Modules:
  0.0 262.2 jit_solution(3415628741420785148)
XLA Ops:
  6.5 0.7 all-gather.5.cloned.1.call-update
  7.3 0.7 all-gather.9.cloned.1.call-update
  8.1 1.2 convolution_bitcast_fusion.1
  11.5 10.7 %all-gather.5.cloned.1.call-done = bf16[4096,256]{1,0:T(8,128)(2,1)} async-done(((bf16[2048,256]{1,0:T(8,128)(2,1)}), bf16[4096,256]{1,0:T(8,128)(2,1)}) %all-gather.5.cloned.1.call-update) | async-done | bytes 2097168 | tf_op jit(solution)/shard_map/all_gather | solution.py:16
  22.2 3.7 %gather_fusion.1 = bf16[32,128,256]{2,1,0:T(8,128)(2,1)} fusion(bf16[32,128,256]{2,1,0:T(8,128)(2,1)} %bitcast.65, s32[1024]{0:T(1024)S(1)} %pad_clamp_fusion), kind=kCustom, calls=%fused_computation.1 | custom fusion | bytes 4194432 | tf_op jit(solution)/shard_map/jit(_take)/gather | solution.py:32
  25.9 1.8 broadcast_select_fusion
  27.7 82.8 %all-gather.9.cloned.1.call-done = bf16[10240,256]{1,0:T(8,128)(2,1)} async-done(((bf16[640,256]{1,0:T(8,128)(2,1)}), bf16[10240,256]{1,0:T(8,128)(2,1)}) %all-gather.9.cloned.1.call-update) | async-done | bytes 5242896 | tf_op jit(solution)/shard_map/all_gather | solution.py:33
  110.5 7.8 %copy.20 = bf16[16,640,256]{2,0,1:T(8,128)(2,1)} copy(bf16[16,640,256]{2,1,0:T(8,128)(2,1)} %bitcast.62) | data formatting | bytes 10485760 | tf_op jit(solution)/shard_map/all_gather | solution.py:33
  118.3 8.9 %reshape_reshape.3 = bf16[10,64,4096]{2,1,0:T(8,128)(2,1)} reshape(bf16[640,16,256]{2,1,0:T(8,128)(2,1)} %bitcast.61) | data formatting | bytes 10485760 | tf_op jit(solution)/shard_map/reshape;reshape | solution.py:35
  127.2 25.2 %while.10 = (s32[]{:T(128)}, bf16[10,64,256]{2,1,0:T(8,128)(2,1)}, bf16[10,64,4096]{2,1,0:T(8,128)(2,1)}, bf16[10,32,2]{1,2,0:T(2,128)(2,1)S(1)}, bf16[32,128,256]{2,1,0:T(8,128)(2,1)S(1)}, /*index=5*/s32[]{:T(128)}) while((s32[]{:T(128)}, bf16[10,64,256]{2,1,0:T(8,128)(2,1)}, bf16[10,64,4096]{2,1,0:T(8,128)(2,1)}, ...), condition=%wide.region_1.2_spmd, body=%wide.region_0.1_spmd.sunk | while | flops 135266304 | bytes 6948561 | solution.py:44
  127.6 2.1 fusion.27
  130.1 2.1 fusion.27
  132.6 2.1 fusion.27
  135.1 2.1 fusion.27
  137.6 2.1 fusion.27
  140.2 2.1 fusion.27
  142.7 2.1 fusion.27
  145.2 2.1 fusion.27
  147.7 2.1 fusion.27
  150.2 2.1 fusion.27
  152.7 97.0 %all-gather.7.cloned.1.call-done = bf16[640,4096]{1,0:T(8,128)(2,1)} async-done(((bf16[640,256]{1,0:T(8,128)(2,1)}), bf16[640,4096]{1,0:T(8,128)(2,1)}) %all-gather.7.cloned.1.call-update) | async-done | bytes 5242896 | tf_op jit(solution)/shard_map/all_gather | solution.py:46
  249.6 4.1 %copy.14 = bf16[80,8,32,128]{3,2,1,0:T(8,128)(2,1)S(1)} copy(bf16[80,8,32,128]{3,1,2,0:T(8,128)(2,1)} %bitcast.63) | data formatting | bytes 10485760
  253.8 0.9 fusion.13
  254.7 0.9 fusion.5
  (73 shorter events, 6.3 us)
Async XLA Ops:
  6.5 145.9 %copy-start = (f32[4096]{0:T(1024)S(1)}, f32[4096]{0:T(1024)}, u32[]{:S(2)}) copy-start(f32[4096]{0:T(1024)} %param.13) | copy-start | bytes 49156
  6.5 15.7 %all-gather.5.cloned.1.call-start = ((), (), s32[]{:S(2)}) async-start(), calls=%async_computation | async-start | bytes 3145728 | tf_op jit(solution)/shard_map/all_gather | solution.py:16
  7.3 103.2 %all-gather.9.cloned.1.call-start = ((), (), s32[]{:S(2)}) async-start(), calls=%async_computation.2 | async-start | bytes 5570560 | tf_op jit(solution)/shard_map/all_gather | solution.py:33
  8.0 241.6 %all-gather.7.cloned.1.call-start = ((), (), s32[]{:S(2)}) async-start(), calls=%async_computation.1 | async-start | bytes 5570560 | tf_op jit(solution)/shard_map/all_gather | solution.py:46
  127.2 25.2 %copy-start.3 = (s32[32]{0:T(128)S(1)}, s32[32]{0:T(128)}, u32[]{:S(2)}) copy-start(s32[32]{0:T(128)} %param.9) | copy-start | bytes 388
  253.8 1.0 copy-start.1
  253.8 1.0 copy-start.2
Sparse Core Ops, SparseCore 0:
  8.9 13.2 all-gather.4
  25.0 85.4 all-gather.8
  152.5 97.0 all-gather.6
